TPU v7x, 32 devices: a whole 2x2x4 slice. The times are simulated.
32 devices in a mesh: dp: 4 (over y, x), space: 8 (over z, core).
Axes of the slice: x: 2, y: 2, z: 4, core: 2. Of those that a mesh axis runs over, the one named last changes fastest.
Arguments:
- signal: bfloat16 [4, 512, 64, 1280], P('dp', None, 'space'), may hold values from -6 to 6
- cotangent: bfloat16 [4, 512, 64, 1280], P('dp', None, 'space'), may hold values from -6 to 6
- spec_weight: bfloat16 [2, 20, 20, 73728], P(None, None, None, 'space'), may hold values from -1.25 to 1.25
- point_weight: bfloat16 [20, 20], replicated, may hold values from -1.25 to 1.25
- bias: bfloat16 [20], replicated, may hold values from -3 to 3
Outputs:
- grad_signal: bfloat16 [4, 512, 64, 1280], P('dp', None, 'space')
- spec_grad: float32 [2, 20, 20, 73728], P(None, None, None, ('space', 'dp'))
All inputs are finite; a program needn't handle non-finite values.
Results may differ from a plain program's by a relative error of at most 0.024.
Values may be sent and summed in bfloat16 or wider, within the bound.
No kernel may reach another device: no remote copies, remote signals or barrier semaphores. Data moves between devices by JAX's collectives and lax.ppermute only.
A program may use at most 256 MiB of HBM per device.

v0:
```python
import math
import jax
import jax.numpy as jnp
from jax import lax
from jax.sharding import PartitionSpec as P

NX = 64
NY = 64
NZ = 32
NT = 16
C = 20
MX = 24
MY = 24
MZ = 16
MT = 8
MZT = 128


def retained(mode_count, length):
    positions = jnp.arange(mode_count, dtype=jnp.int32)
    return jnp.where(positions < mode_count // 2, positions, length - mode_count + positions)


def complex_table(mode_count, length):
    freqs = retained(mode_count, length)
    points = jnp.arange(length, dtype=jnp.int32)
    turns = freqs[:, None] * points[None, :] % length
    angles = turns.astype(jnp.float32) * (2.0 * math.pi / length)
    norm_scale = 1.0 / math.sqrt(length)
    cos_part = jnp.cos(angles) * norm_scale
    sin_part = jnp.sin(angles) * norm_scale
    upper_rows = jnp.stack([cos_part, sin_part], axis=1)
    lower_rows = jnp.stack([-sin_part, cos_part], axis=1)
    return jnp.stack([upper_rows, lower_rows], axis=0).astype(jnp.bfloat16)


def depth_tables():
    depth_freq = retained(MZ, NZ)
    time_freq = jnp.arange(MT, dtype=jnp.int32)
    depth_pos = jnp.arange(NZ, dtype=jnp.int32)
    time_pos = jnp.arange(NT, dtype=jnp.int32)
    depth_turns = depth_freq[:, None] * depth_pos[None, :] % NZ
    time_turns = time_freq[:, None] * time_pos[None, :] % NT
    turns = depth_turns[:, None, :, None] * NT + time_turns[None, :, None, :] * NZ
    angles = turns.astype(jnp.float32) * (2.0 * math.pi / (NZ * NT))
    norm_scale = 1.0 / math.sqrt(NZ * NT)
    forward = jnp.stack([jnp.cos(angles), -jnp.sin(angles)], axis=2) * norm_scale
    doubling = jnp.where(time_freq == 0, 1.0, 2.0).astype(jnp.float32)
    inverse = forward * doubling[None, :, None, None, None]
    return (
        forward.reshape(MZT, 2, NZ * NT).astype(jnp.bfloat16),
        inverse.reshape(MZT, 2, NZ * NT).astype(jnp.bfloat16),
    )


def gelu_slope(pre_act):
    cumulative = 0.5 * (1.0 + lax.erf(pre_act * (1.0 / math.sqrt(2.0))))
    density = jnp.exp(-0.5 * pre_act * pre_act) * (1.0 / math.sqrt(2.0 * math.pi))
    return cumulative + pre_act * density


def block_tables(table_y):
    identity = jnp.eye(C, dtype=jnp.float32)
    wide = table_y.astype(jnp.float32)
    rows = []
    for part_in in range(2):
        row = []
        for part_out in range(2):
            block = jnp.einsum("cd,jy->cydj", identity, wide[part_out, :, part_in, :])
            row.append(block.reshape(C * NY, C * MY).astype(jnp.bfloat16))
        rows.append(row)
    return rows


def forward_y(blocks, real_in, imag_in):
    outputs = []
    for part_out in range(2):
        total = jnp.einsum(
            "smxr,rK->smxK", real_in, blocks[0][part_out], preferred_element_type=jnp.float32
        ) + jnp.einsum(
            "smxr,rK->smxK", imag_in, blocks[1][part_out], preferred_element_type=jnp.float32
        )
        outputs.append(total.astype(jnp.bfloat16))
    return (outputs[0], outputs[1])


def inverse_y(blocks, real_in, imag_in):
    outputs = []
    for part_out in range(2):
        total = jnp.einsum(
            "smxK,rK->smxr", real_in, blocks[part_out][0], preferred_element_type=jnp.float32
        ) + jnp.einsum(
            "smxK,rK->smxr", imag_in, blocks[part_out][1], preferred_element_type=jnp.float32
        )
        outputs.append(total.astype(jnp.bfloat16))
    return (outputs[0], outputs[1])


def forward_x(table_x, real_in, imag_in):
    samples, modes_here, cells, merged = real_in.shape
    total = jnp.einsum(
        "Pix,smxr->sPmir", table_x[:, :, 0, :], real_in, preferred_element_type=jnp.float32
    ) + jnp.einsum(
        "Pix,smxr->sPmir", table_x[:, :, 1, :], imag_in, preferred_element_type=jnp.float32
    )
    rounded = total.astype(jnp.bfloat16).reshape(samples, 2, modes_here, MX, C, MY)
    return jnp.transpose(rounded, (0, 1, 4, 2, 3, 5)).reshape(samples, 2, C, modes_here * MX * MY)


def inverse_x(table_x, spectrum):
    samples = spectrum.shape[0]
    unmerged = spectrum.reshape(samples, 2, C, -1, MX, MY)
    modes_here = unmerged.shape[3]
    moved = jnp.transpose(unmerged, (0, 1, 3, 4, 2, 5)).reshape(samples, 2, modes_here, MX, C * MY)
    real_out = jnp.einsum(
        "Pix,sPmir->smxr", table_x[:, :, 0, :], moved, preferred_element_type=jnp.float32
    )
    imag_out = jnp.einsum(
        "Pix,sPmir->smxr", table_x[:, :, 1, :], moved, preferred_element_type=jnp.float32
    )
    return (real_out.astype(jnp.bfloat16), imag_out.astype(jnp.bfloat16))


def analyse(blocks, table_x, coeffs):
    samples, rows_all, cells, merged = coeffs.shape
    split = coeffs.reshape(samples, MZT, 2, cells, merged)
    moved = lax.all_to_all(split, "space", split_axis=1, concat_axis=3, tiled=True)
    real_m, imag_m = forward_y(blocks, moved[:, :, 0], moved[:, :, 1])
    return forward_x(table_x, real_m, imag_m)


def synthesise(blocks, table_x, spectrum):
    real_x, imag_x = inverse_x(table_x, spectrum)
    real_y, imag_y = inverse_y(blocks, real_x, imag_x)
    real_out, imag_out = (
        lax.all_to_all(real_y, "space", split_axis=2, concat_axis=1, tiled=True),
        lax.all_to_all(imag_y, "space", split_axis=2, concat_axis=1, tiled=True),
    )
    return (real_out, imag_out)


def to_grid(table, real_in, imag_in):
    return jnp.einsum(
        "mz,smxr->szxr", table[:, 0, :], real_in, preferred_element_type=jnp.float32
    ) + jnp.einsum("mz,smxr->szxr", table[:, 1, :], imag_in, preferred_element_type=jnp.float32)


def weight_terms(u_hat, h_hat):
    real_part = jnp.einsum(
        "gsik,gsok->giok", u_hat[:, :, 0], h_hat[:, :, 0], preferred_element_type=jnp.float32
    ) + jnp.einsum(
        "gsik,gsok->giok", u_hat[:, :, 1], h_hat[:, :, 1], preferred_element_type=jnp.float32
    )
    imag_part = jnp.einsum(
        "gsik,gsok->giok", u_hat[:, :, 0], h_hat[:, :, 1], preferred_element_type=jnp.float32
    ) - jnp.einsum(
        "gsik,gsok->giok", u_hat[:, :, 1], h_hat[:, :, 0], preferred_element_type=jnp.float32
    )
    return jnp.stack([real_part, imag_part], axis=1)


def local(signal, cotangent, spec_weight, point_weight, bias):
    samples, depth_len, x_rows, merged = signal.shape
    depth_table, depth_inverse = depth_tables()
    table_y = complex_table(MY, NY)
    table_x = complex_table(MX, NX)
    blocks = block_tables(table_y)
    point_block = (
        jnp.einsum("co,yz->cyoz", point_weight.astype(jnp.float32), jnp.eye(NY, dtype=jnp.float32))
        .reshape(C * NY, C * NY)
        .astype(jnp.bfloat16)
    )
    bias_row = jnp.repeat(bias.astype(jnp.float32), NY)
    w_real = spec_weight[0]
    w_imag = spec_weight[1]
    forward_flat = depth_table.reshape(2 * MZT, depth_len)
    inverse_flat = depth_inverse.reshape(2 * MZT, depth_len)
    coeffs = jnp.einsum(
        "qz,szxr->sqxr", forward_flat, signal, preferred_element_type=jnp.float32
    ).astype(jnp.bfloat16)
    u_hat = analyse(blocks, table_x, coeffs)
    v_real = jnp.einsum(
        "sik,iok->sok", u_hat[:, 0], w_real, preferred_element_type=jnp.float32
    ) - jnp.einsum("sik,iok->sok", u_hat[:, 1], w_imag, preferred_element_type=jnp.float32)
    v_imag = jnp.einsum(
        "sik,iok->sok", u_hat[:, 1], w_real, preferred_element_type=jnp.float32
    ) + jnp.einsum("sik,iok->sok", u_hat[:, 0], w_imag, preferred_element_type=jnp.float32)
    v_hat = jnp.stack([v_real, v_imag], axis=1).astype(jnp.bfloat16)
    real_syn, imag_syn = synthesise(blocks, table_x, v_hat)
    spectral = to_grid(depth_inverse, real_syn, imag_syn)
    direct = jnp.einsum("szxr,rR->szxR", signal, point_block, preferred_element_type=jnp.float32)
    pre_act = spectral + direct + bias_row
    hidden = (cotangent.astype(jnp.float32) * gelu_slope(pre_act)).astype(jnp.bfloat16)
    e_coeffs = jnp.einsum(
        "qz,szxr->sqxr", inverse_flat, hidden, preferred_element_type=jnp.float32
    ).astype(jnp.bfloat16)
    h_hat = analyse(blocks, table_x, e_coeffs)
    d_real = jnp.einsum(
        "sok,iok->sik", h_hat[:, 0], w_real, preferred_element_type=jnp.float32
    ) + jnp.einsum("sok,iok->sik", h_hat[:, 1], w_imag, preferred_element_type=jnp.float32)
    d_imag = jnp.einsum(
        "sok,iok->sik", h_hat[:, 1], w_real, preferred_element_type=jnp.float32
    ) - jnp.einsum("sok,iok->sik", h_hat[:, 0], w_imag, preferred_element_type=jnp.float32)
    d_hat = jnp.stack([d_real, d_imag], axis=1).astype(jnp.bfloat16)
    real_back, imag_back = synthesise(blocks, table_x, d_hat)
    returned = to_grid(depth_table, real_back, imag_back)
    pointwise = jnp.einsum("szxR,rR->szxr", hidden, point_block, preferred_element_type=jnp.float32)
    grad_signal = (returned + pointwise).astype(jnp.bfloat16)
    partial_value = weight_terms(u_hat[None], h_hat[None])[0]
    spec_grad = lax.psum_scatter(
        partial_value.astype(jnp.bfloat16), "dp", scatter_dimension=3, tiled=True
    ).astype(jnp.float32)
    return (grad_signal, spec_grad)


def solution(mesh):
    return jax.shard_map(
        local,
        mesh=mesh,
        in_specs=(
            P("dp", None, "space", None),
            P("dp", None, "space", None),
            P(None, None, None, "space"),
            P(),
            P(),
        ),
        out_specs=(P("dp", None, "space", None), P(None, None, None, ("space", "dp"))),
        check_vma=False,
    )
```

profile of v0, /device:TPU:0, one launch (start us, length us, event | category | flops | bytes accessed | tf_op | source)
XLA Modules:
  0.0 866.7 jit_solution(4177913953414593239)
XLA Ops:
  7.4 8.9 %sine_negate_fusion = (f32[16,8,32,16]{3,2,1,0:T(8,128)}, f32[16,8,32,16]{3,2,1,0:T(8,128)S(1)}) fusion(s32[8,16]{1,0:T(8,128)S(1)} %fusion.101, s32[16,32]{1,0:T(8,128)S(1)} %fusion.90), kind=kLoop, calls=%fused_computation.94 | loop fusion | flops 262144 | bytes 526848 | tf_op jit(solution)/shard_map/neg | solution.py:47
  22.9 7.9 fusion.27
  36.0 6.6 all-to-all-start
  63.5 29.8 %fusion.106 = (bf16[1,20,20,9216]{3,0,2,1:T(2,128)(2,1)}, bf16[1,20,20,9216]{3,0,2,1:T(2,128)(2,1)}) fusion(bf16[2,20,20,9216]{3,0,2,1:T(2,128)(2,1)} %param.7), kind=kLoop, calls=%fused_computation.200 | loop fusion | bytes 29491200 | tf_op jit(solution)/shard_map/slice | solution.py:175
  93.3 65.8 %all-to-all-done = bf16[1,128,2,8,1280]{4,3,2,0,1:T(8,128)(2,1)} async-done(((bf16[1,128,2,8,1280]{4,3,2,0,1:T(8,128)(2,1)}), bf16[1,128,2,8,1280]{4,3,2,0,1:T(8,128)(2,1)}, u32[]{:S(2)}, u32[]{:S(2)}) %all-to-all-start) | async-done | bytes 5242912 | tf_op jit(solution)/shard_map/all_to_all | solution.py:127
  190.4 6.5 reshape.685
  198.3 19.7 %fusion.8 = (f32[9216,20]{0,1:T(8,128)S(1)}, f32[9216,20]{0,1:T(8,128)S(1)}, f32[9216,20]{0,1:T(8,128)S(1)}, f32[9216,20]{0,1:T(8,128)}) fusion(f32[9216,20]{0,1:T(8,128)S(1)} %get-tuple-element.57, bf16[1,20,20,9216]{3,0,2,1:T(2,128)(2,1)} %get-tuple-element.25, f32[9216,20]{0,1:T(8,128)S(1)} %get-tuple-element.56, ...), kind=kLoop, calls=%fused_computation.19 | loop fusion | flops 36126720 | bytes 19169280 | tf_op jit(solution)/shard_map/sik,iok->sok/dot_general | solution.py:182
  233.8 6.4 copy.144
  240.2 6.3 reshape.688
  268.4 53.0 %all-to-all-done.2 = bf16[1,16,64,1280]{3,1,0,2:T(8,128)(2,1)} async-done(((bf16[1,16,64,1280]{3,1,0,2:T(8,128)(2,1)}), bf16[1,16,64,1280]{3,1,0,2:T(8,128)(2,1)}, u32[]{:S(2)}, u32[]{:S(2)}) %all-to-all-start.2) | async-done | bytes 2621472 | tf_op jit(solution)/shard_map/all_to_all | solution.py:137
  331.5 10.0 %convert_element_type.327 = bf16[1280,1280]{1,0:T(8,128)(2,1)} reshape(bf16[20,64,20,64]{3,2,1,0:T(8,128)(2,1)} %fusion.23) | data formatting | bytes 6553600 | tf_op jit(solution)/shard_map/convert_element_type | solution.py:171
  341.4 16.4 %copy.132 = bf16[1,512,8,1280]{1,3,2,0:T(8,128)(2,1)} copy(bf16[1,512,8,1280]{3,2,1,0:T(8,128)(2,1)} %param.6) | data formatting | bytes 20971520 | tf_op args[1]
  357.8 21.6 %fusion.17 = f32[1280,512,8]{1,0,2:T(8,128)} fusion(bf16[512,8,1280]{2,1,0:T(8,128)(2,1)} %bitcast.477, bf16[1280,1280]{1,0:T(8,128)(2,1)} %convert_element_type.327), kind=kOutput, calls=%fused_computation.32 | convolution fusion | flops 13421772800 | bytes 34734080 | tf_op jit(solution)/shard_map/szxr,rR->szxR/dot_general | solution.py:191
  389.0 9.0 %fusion.44 = f32[8,1280,512]{2,1,0:T(8,128)} fusion(bf16[128,8,1280]{2,1,0:T(8,128)(2,1)S(1)} %bitcast.458, bf16[128,2,512]{2,0,1:T(8,128)(2,1)S(1)} %copy-done.18), kind=kOutput, calls=%fused_computation.75 | convolution fusion | flops 1342177280 | bytes 23724032 | tf_op jit(solution)/shard_map/mz,smxr->szxr/dot_general | solution.py:143
  398.0 21.2 %fusion.16 = bf16[512,8,1280]{0,2,1:T(8,128)(2,1)S(1)} fusion(f32[1280,512,8]{1,0,2:T(8,128)} %fusion.17, f32[8,1280,512]{2,1,0:T(8,128)} %fusion.44, bf16[1,512,8,1280]{1,3,2,0:T(8,128)(2,1)} %copy.132, f32[1280]{0:T(1024)S(1)} %add.243, bf16[128,8,1280]{2,1,0:T(8,128)(2,1)} %bitcast.475, bf16[128,2,512]{2,0,1:T(8,128)(2,1)S(1)} %copy-done.18), kind=kOutput, calls=%fused_computation.31 | convolution fusion | flops 1415577600 | bytes 65675264 | tf_op jit(solution)/shard_map/mz,smxr->szxr/dot_general | solution.py:145
  433.3 6.3 broadcast_in_dim_reshape.8
  442.2 107.5 %all-to-all-done.3 = bf16[1,128,2,8,1280]{4,3,2,0,1:T(8,128)(2,1)} async-done(((bf16[1,128,2,8,1280]{4,3,2,0,1:T(8,128)(2,1)}), bf16[1,128,2,8,1280]{4,3,2,0,1:T(8,128)(2,1)}, u32[]{:S(2)}, u32[]{:S(2)}) %all-to-all-start.3) | async-done | bytes 5242912 | tf_op jit(solution)/shard_map/all_to_all | solution.py:127
  564.3 5.9 fusion.66
  581.1 6.2 broadcast_in_dim_reshape.7
  594.5 8.7 %maximum_bitcast_fusion = bf16[2,20,20,9216]{3,2,1,0:T(8,128)(2,1)} fusion(bf16[1,1,20,20,9216]{4,3,2,1,0:T(8,128)(2,1)S(1)} %get-tuple-element.27, bf16[1,1,20,20,9216]{4,3,2,1,0:T(8,128)(2,1)S(1)} %get-tuple-element.26), kind=kLoop, calls=%fused_computation.27 | loop fusion | flops 7372800 | bytes 29491200 | tf_op jit(solution)/shard_map/convert_element_type | solution.py:211
  603.2 6.2 reshape.698
  610.7 23.0 %fusion.12 = (f32[9216,20]{0,1:T(8,128)S(1)}, f32[9216,20]{0,1:T(8,128)S(1)}, f32[9216,20]{0,1:T(8,128)S(1)}, f32[9216,20]{0,1:T(8,128)}) fusion(f32[9216,20]{0,1:T(8,128)S(1)} %bitcast_convert_fusion.5, bf16[1,20,20,9216]{3,0,2,1:T(2,128)(2,1)} %get-tuple-element.25, f32[9216,20]{0,1:T(8,128)S(1)} %bitcast_convert_fusion.4, ...), kind=kLoop, calls=%fused_computation.23 | loop fusion | flops 36126720 | bytes 19169280 | tf_op jit(solution)/shard_map/sok,iok->sik/dot_general | solution.py:198
  650.1 6.4 copy.163
  656.5 6.6 reshape.701
  683.8 54.3 %all-to-all-done.5 = bf16[1,16,64,1280]{3,1,0,2:T(8,128)(2,1)} async-done(((bf16[1,16,64,1280]{3,1,0,2:T(8,128)(2,1)}), bf16[1,16,64,1280]{3,1,0,2:T(8,128)(2,1)}, u32[]{:S(2)}, u32[]{:S(2)}) %all-to-all-start.5) | async-done | bytes 2621472 | tf_op jit(solution)/shard_map/all_to_all | solution.py:137
  742.7 8.8 %reshape.756 = bf16[1280,1280,1]{1,0,2:T(8,128)(2,1)S(1)} reshape(bf16[20,64,20,64]{3,2,1,0:T(8,128)(2,1)} %fusion.23) | data formatting | bytes 6553600 | tf_op jit(solution)/shard_map/convert_element_type | solution.py:171
  751.6 20.5 %fusion.113 = f32[512,8,1280]{0,2,1:T(8,128)} fusion(bf16[1280,1280,1]{1,0,2:T(8,128)(2,1)S(1)} %reshape.756, bf16[512,8,1280]{0,2,1:T(8,128)(2,1)} %copy-done), kind=kOutput, calls=%fused_computation.207 | convolution fusion | flops 13421772800 | bytes 34734080 | tf_op jit(solution)/shard_map/szxR,rR->szxr/dot_general | solution.py:207
  774.7 28.3 %all-to-all-done.4 = bf16[1,16,64,1280]{3,1,0,2:T(8,128)(2,1)} async-done(((bf16[1,16,64,1280]{3,1,0,2:T(8,128)(2,1)}), bf16[1,16,64,1280]{3,1,0,2:T(8,128)(2,1)}, u32[]{:S(2)}, u32[]{:S(2)}) %all-to-all-start.4) | async-done | bytes 2621472 | tf_op jit(solution)/shard_map/all_to_all | solution.py:136
  806.5 8.6 fusion.41
  815.1 18.5 %fusion.6 = bf16[1,512,8,1280]{1,3,2,0:T(8,128)(2,1)} fusion(f32[512,8,1280]{0,2,1:T(8,128)} %fusion.113, f32[8,1280,512]{2,1,0:T(8,128)} %fusion.41, bf16[128,8,1280]{2,1,0:T(8,128)(2,1)S(1)} %bitcast.460, bf16[128,2,512]{2,0,1:T(8,128)(2,1)S(1)} %copy-done.17), kind=kOutput, calls=%fused_computation.16 | convolution fusion | flops 1357905920 | bytes 55181312 | tf_op jit(solution)/shard_map/mz,smxr->szxr/dot_general | solution.py:145
  833.6 16.9 %copy.176 = bf16[1,512,8,1280]{3,2,1,0:T(8,128)(2,1)} copy(bf16[1,512,8,1280]{1,3,2,0:T(8,128)(2,1)} %fusion.6) | data formatting | bytes 20971520
  850.5 9.1 %copy.177 = f32[2,20,20,2304]{3,0,2,1:T(2,128)} copy(bf16[2,20,20,2304]{3,2,1,0:T(8,128)(2,1)} %reduce-scatter.2.cloned.1.call-done) | data formatting | bytes 11059200
  (146 shorter events, 220.8 us)
Async XLA Ops:
  21.8 0.7 copy-start.16
  36.0 123.1 %all-to-all-start = ((bf16[1,128,2,8,1280]{4,3,2,0,1:T(8,128)(2,1)}), bf16[1,128,2,8,1280]{4,3,2,0,1:T(8,128)(2,1)}, u32[]{:S(2)}, u32[]{:S(2)}) async-start(bf16[1,128,2,8,1280]{4,3,2,0,1:T(8,128)(2,1)} %bitcast.454), calls=%async_computation | async-start | bytes 10485760 | tf_op jit(solution)/shard_map/all_to_all | solution.py:127
  159.1 3.2 copy-start.1
  162.3 3.1 copy-start.12
  162.4 3.0 copy-start.3
  165.4 2.9 copy-start.2
  249.7 1.0 copy-start.11
  250.7 1.5 copy-start.7
  256.7 64.7 %all-to-all-start.2 = ((bf16[1,16,64,1280]{3,1,0,2:T(8,128)(2,1)}), bf16[1,16,64,1280]{3,1,0,2:T(8,128)(2,1)}, u32[]{:S(2)}, u32[]{:S(2)}) async-start(bf16[1,16,64,1280]{3,1,0,2:T(8,128)(2,1)} %copy.149), calls=%async_computation.2 | async-start | bytes 5242880 | tf_op jit(solution)/shard_map/all_to_all | solution.py:137
  261.1 2.9 copy-start.4
  268.4 57.6 %copy-start.19 = (bf16[20,20]{1,0:T(8,128)(2,1)S(1)}, bf16[20,20]{1,0:T(8,128)(2,1)}, u32[]{:S(2)}) copy-start(bf16[20,20]{1,0:T(8,128)(2,1)} %param.8) | copy-start | bytes 2404
  268.4 57.7 %copy-start.20 = (bf16[20]{0:T(256)(128)(2,1)S(1)}, bf16[20]{0:T(256)(128)(2,1)}, u32[]{:S(2)}) copy-start(bf16[20]{0:T(256)(128)(2,1)} %param.9) | copy-start | bytes 124
  268.4 57.8 %copy-start.18 = (bf16[128,2,512]{2,0,1:T(8,128)(2,1)S(1)}, bf16[128,2,512]{2,0,1:T(8,128)(2,1)}, u32[]{:S(2)}) copy-start(bf16[128,2,512]{2,0,1:T(8,128)(2,1)} %get-tuple-element.36) | copy-start | bytes 786436
  321.4 64.9 %all-to-all-start.1 = ((bf16[1,16,64,1280]{3,1,0,2:T(8,128)(2,1)}), bf16[1,16,64,1280]{3,1,0,2:T(8,128)(2,1)}, u32[]{:S(2)}, u32[]{:S(2)}) async-start(bf16[1,16,64,1280]{3,1,0,2:T(8,128)(2,1)} %copy.145), calls=%async_computation.1 | async-start | bytes 5242880 | tf_op jit(solution)/shard_map/all_to_all | solution.py:136
  419.3 4.1 copy-start
  428.6 121.1 %all-to-all-start.3 = ((bf16[1,128,2,8,1280]{4,3,2,0,1:T(8,128)(2,1)}), bf16[1,128,2,8,1280]{4,3,2,0,1:T(8,128)(2,1)}, u32[]{:S(2)}, u32[]{:S(2)}) async-start(bf16[1,128,2,8,1280]{4,3,2,0,1:T(8,128)(2,1)} %bitcast.455), calls=%async_computation.3 | async-start | bytes 10485760 | tf_op jit(solution)/shard_map/all_to_all | solution.py:127
  433.3 417.2 %reduce-scatter.2.cloned.1.call-start = ((), (), s32[]{:S(2)}) async-start(), calls=%async_computation.7 | async-start | bytes 22118400 | tf_op jit(solution)/shard_map/reduce_scatter | solution.py:210
  549.7 3.2 copy-start.5
  553.0 3.1 copy-start.13
  587.3 1.3 copy-start.14
  587.3 1.4 copy-start.15
  666.4 1.0 copy-start.9
  667.3 1.5 copy-start.8
  670.4 7.4 copy-start.10
  673.4 64.7 %all-to-all-start.5 = ((bf16[1,16,64,1280]{3,1,0,2:T(8,128)(2,1)}), bf16[1,16,64,1280]{3,1,0,2:T(8,128)(2,1)}, u32[]{:S(2)}, u32[]{:S(2)}) async-start(bf16[1,16,64,1280]{3,1,0,2:T(8,128)(2,1)} %copy.168), calls=%async_computation.5 | async-start | bytes 5242880 | tf_op jit(solution)/shard_map/all_to_all | solution.py:137
  677.8 1.5 copy-start.6
  738.1 64.9 %all-to-all-start.4 = ((bf16[1,16,64,1280]{3,1,0,2:T(8,128)(2,1)}), bf16[1,16,64,1280]{3,1,0,2:T(8,128)(2,1)}, u32[]{:S(2)}, u32[]{:S(2)}) async-start(bf16[1,16,64,1280]{3,1,0,2:T(8,128)(2,1)} %copy.164), calls=%async_computation.4 | async-start | bytes 5242880 | tf_op jit(solution)/shard_map/all_to_all | solution.py:136
  805.5 1.0 copy-start.17
Sparse Core Ops, SparseCore 0:
  603.3 160.1 reduce-scatter.1
where the time goes:
time: 878 us; the launch traced here: 867 us
  waiting for transfers between devices  312 us (36%)
  local copies, waits for them, and re-layouts  255 us (29%)
  matrix products  165 us (19%)
  other arithmetic  91.1 us (10%)
  starting transfers between devices  29.3 us (3%)
  between operations  15 us (2%)
    all_to_all x2, waiting for transfers between devices, analyse(): lax.all_to_all(split, 'space', split_axis=1, concat_axis=3, tiled=True)  173 us
    all_to_all x2, waiting for transfers between devices, synthesise(): lax.all_to_all(imag_y, 'space', split_axis=2, concat_axis=1, tiled=True)  107 us
    unnamed x48, local copies, waits for them, and re-layouts  46.9 us
    dot_general x2, matrix products, to_grid(): jnp.einsum('mz,smxr->szxr', table[:, 1, :], imag_in, preferred_element_ty...  39.7 us
    all_to_all x2, waiting for transfers between devices, synthesise(): lax.all_to_all(real_y, 'space', split_axis=2, concat_axis=1, tiled=True)  30.9 us
    slice x1, local copies, waits for them, and re-layouts, local(): w_imag = spec_weight[1]  29.8 us
    dot_general x1, other arithmetic, local(): jnp.einsum('sok,iok->sik', h_hat[:, 0], w_real, preferred_element_type=jn...  23 us
    dot_general x1, matrix products, local(): jnp.einsum('szxr,rR->szxR', signal, point_block, preferred_element_type=j...  21.6 us
  transfers between devices with their start and end apart: 7, of which 6 were waited for; matrix products, arithmetic and copies ran while one was open for 32% of the time, Pallas kernels for 0%

commit v1 on v0

--- a/solution.py
+++ b/solution.py
@@ -124,7 +124,10 @@
 def analyse(blocks, table_x, coeffs):
     samples, rows_all, cells, merged = coeffs.shape
     split = coeffs.reshape(samples, MZT, 2, cells, merged)
-    moved = lax.all_to_all(split, "space", split_axis=1, concat_axis=3, tiled=True)
+    moved = jnp.concatenate(
+        lax.all_to_all(jnp.stack(jnp.split(split, lax.axis_size("space"), axis=1)), "space", 0, 0),
+        axis=3,
+    )
     real_m, imag_m = forward_y(blocks, moved[:, :, 0], moved[:, :, 1])
     return forward_x(table_x, real_m, imag_m)
 

time: 878 us -> 939 us (1.069)
  local copies, waits for them, and re-layouts: 255 us -> 312 us
    unnamed x48 -> x60, local copies, waits for them, and re-layouts: 46.9 us -> 82.7 us
    reshape x2, local copies, waits for them, and re-layouts: 10.5 us -> 22.7 us  [analyse(): split = coeffs.reshape(samples, MZT, 2, cells, merged)]
    reshape x0 -> x2, local copies, waits for them, and re-layouts: none -> 11 us  [analyse(): jnp.concatenate(lax.all_to_all(jnp.stack(jnp.split(split, lax.axis_size('...]
    another operation x3 -> x5, local copies, waits for them, and re-layouts: 14.4 us -> 19 us
  transfers between devices with their start and end apart: 7 -> 7, of which waited for: 6 -> 6; matrix products, arithmetic and copies ran while one was open for 32% -> 30% of each run, Pallas kernels for 0% -> 0%
where the time goes in v1:
time: 939 us; the launch traced here: 928 us
  local copies, waits for them, and re-layouts  312 us (33%)
  waiting for transfers between devices  310 us (33%)
  matrix products  170 us (18%)
  other arithmetic  91.3 us (10%)
  starting transfers between devices  29.7 us (3%)
  between operations  14.9 us (2%)
    all_to_all x2, waiting for transfers between devices, analyse(): lax.all_to_all(jnp.stack(jnp.split(split, lax.axis_size('space'), axis=1)...  173 us
    all_to_all x2, waiting for transfers between devices, synthesise(): lax.all_to_all(imag_y, 'space', split_axis=2, concat_axis=1, tiled=True)  106 us
    unnamed x60, local copies, waits for them, and re-layouts  82.7 us
    dot_general x2, matrix products, to_grid(): jnp.einsum('mz,smxr->szxr', table[:, 1, :], imag_in, preferred_element_ty...  39.7 us
    all_to_all x2, waiting for transfers between devices, synthesise(): lax.all_to_all(real_y, 'space', split_axis=2, concat_axis=1, tiled=True)  31 us
    slice x1, local copies, waits for them, and re-layouts, local(): w_imag = spec_weight[1]  30.3 us
    dot_general x1, other arithmetic, local(): jnp.einsum('sok,iok->sik', h_hat[:, 0], w_real, preferred_element_type=jn...  23.1 us
    reshape x2, local copies, waits for them, and re-layouts, analyse(): split = coeffs.reshape(samples, MZT, 2, cells, merged)  22.7 us
  transfers between devices with their start and end apart: 7, of which 6 were waited for; matrix products, arithmetic and copies ran while one was open for 30% of the time, Pallas kernels for 0%

profile of v1, /device:TPU:0, one launch (start us, length us, event | category | flops | bytes accessed | tf_op | source)
XLA Modules:
  0.0 928.1 jit_solution(15076940650242937965)
XLA Ops:
  7.4 8.9 sine_negate_fusion
  22.9 10.2 %fusion.27 = bf16[1,256,8,1280]{3,1,2,0:T(8,128)(2,1)} fusion(bf16[256,512,1]{1,0,2:T(8,128)(2,1)S(1)} %reshape.735, bf16[512,8,1280]{2,1,0:T(8,128)(2,1)} %bitcast.532), kind=kOutput, calls=%fused_computation.51 | convolution fusion | flops 2686976000 | bytes 15990784 | tf_op jit(solution)/shard_map/qz,szxr->sqxr/dot_general | solution.py:181
  33.1 11.5 %reshape.689 = bf16[1,128,2,8,1280]{4,2,1,3,0:T(2,128)(2,1)} reshape(bf16[1,256,8,1280]{3,1,2,0:T(8,128)(2,1)} %fusion.27) | data formatting | bytes 10485760 | tf_op jit(solution)/shard_map/reshape | solution.py:126
  63.6 6.3 all-to-all-start
  90.8 30.3 %fusion.122 = (bf16[1,20,20,9216]{3,0,2,1:T(2,128)(2,1)}, bf16[1,20,20,9216]{3,0,2,1:T(2,128)(2,1)}) fusion(bf16[2,20,20,9216]{3,0,2,1:T(2,128)(2,1)} %param.7), kind=kLoop, calls=%fused_computation.232 | loop fusion | bytes 29491200 | tf_op jit(solution)/shard_map/slice | solution.py:178
  121.2 65.3 %all-to-all-done = bf16[8,1,16,2,8,1280]{5,3,2,4,1,0:T(2,128)(2,1)} async-done(((bf16[8,1,16,2,8,1280]{5,3,2,4,1,0:T(2,128)(2,1)}), bf16[8,1,16,2,8,1280]{5,3,2,4,1,0:T(2,128)(2,1)}, u32[]{:S(2)}, u32[]{:S(2)}) %all-to-all-start) | async-done | bytes 5242912 | tf_op jit(solution)/shard_map/all_to_all | solution.py:128
  227.6 19.9 %fusion.8 = (f32[9216,20]{0,1:T(8,128)S(1)}, f32[9216,20]{0,1:T(8,128)S(1)}, f32[9216,20]{0,1:T(8,128)S(1)}, f32[9216,20]{0,1:T(8,128)}) fusion(f32[9216,20]{0,1:T(8,128)S(1)} %get-tuple-element.57, bf16[1,20,20,9216]{3,0,2,1:T(2,128)(2,1)} %get-tuple-element.25, f32[9216,20]{0,1:T(8,128)S(1)} %get-tuple-element.56, ...), kind=kLoop, calls=%fused_computation.19 | loop fusion | flops 36126720 | bytes 19169280 | tf_op jit(solution)/shard_map/sik,iok->sok/dot_general | solution.py:185
  263.3 6.4 copy.131
  269.8 6.3 reshape.702
  298.1 53.0 %all-to-all-done.2 = bf16[1,16,64,1280]{3,1,0,2:T(8,128)(2,1)} async-done(((bf16[1,16,64,1280]{3,1,0,2:T(8,128)(2,1)}), bf16[1,16,64,1280]{3,1,0,2:T(8,128)(2,1)}, u32[]{:S(2)}, u32[]{:S(2)}) %all-to-all-start.2) | async-done | bytes 2621472 | tf_op jit(solution)/shard_map/all_to_all | solution.py:140
  361.4 10.0 %convert_element_type.327 = bf16[1280,1280]{1,0:T(8,128)(2,1)} reshape(bf16[20,64,20,64]{3,2,1,0:T(8,128)(2,1)} %fusion.23) | data formatting | bytes 6553600 | tf_op jit(solution)/shard_map/convert_element_type | solution.py:174
  371.3 16.4 %copy.122 = bf16[1,512,8,1280]{1,3,2,0:T(8,128)(2,1)} copy(bf16[1,512,8,1280]{3,2,1,0:T(8,128)(2,1)} %param.6) | data formatting | bytes 20971520 | tf_op args[1]
  387.7 21.6 %fusion.17 = f32[1280,512,8]{1,0,2:T(8,128)} fusion(bf16[512,8,1280]{2,1,0:T(8,128)(2,1)} %bitcast.533, bf16[1280,1280]{1,0:T(8,128)(2,1)} %convert_element_type.327), kind=kOutput, calls=%fused_computation.32 | convolution fusion | flops 13421772800 | bytes 34734080 | tf_op jit(solution)/shard_map/szxr,rR->szxR/dot_general | solution.py:194
  418.9 8.8 fusion.44
  427.7 21.3 %fusion.16 = bf16[512,8,1280]{0,2,1:T(8,128)(2,1)S(1)} fusion(f32[1280,512,8]{1,0,2:T(8,128)} %fusion.17, f32[8,1280,512]{2,1,0:T(8,128)} %fusion.44, bf16[1,512,8,1280]{1,3,2,0:T(8,128)(2,1)} %copy.122, f32[1280]{0:T(1024)S(1)} %add.243, bf16[128,8,1280]{2,1,0:T(8,128)(2,1)} %bitcast.531, bf16[128,2,512]{2,0,1:T(8,128)(2,1)S(1)} %copy-done.17), kind=kOutput, calls=%fused_computation.31 | convolution fusion | flops 1415577600 | bytes 65675264 | tf_op jit(solution)/shard_map/mz,smxr->szxr/dot_general | solution.py:148
  458.0 11.2 %reshape.708 = bf16[1,128,2,8,1280]{4,2,1,3,0:T(2,128)(2,1)} reshape(bf16[1,256,8,1280]{3,1,2,0:T(8,128)(2,1)} %fusion.30) | data formatting | bytes 10485760 | tf_op jit(solution)/shard_map/reshape | solution.py:126
  492.9 6.4 broadcast_in_dim_reshape.8
  501.8 107.5 %all-to-all-done.3 = bf16[8,1,16,2,8,1280]{5,3,2,4,1,0:T(2,128)(2,1)} async-done(((bf16[8,1,16,2,8,1280]{5,3,2,4,1,0:T(2,128)(2,1)}), bf16[8,1,16,2,8,1280]{5,3,2,4,1,0:T(2,128)(2,1)}, u32[]{:S(2)}, u32[]{:S(2)}) %all-to-all-start.3) | async-done | bytes 5242912 | tf_op jit(solution)/shard_map/all_to_all | solution.py:128
  643.0 6.5 broadcast_in_dim_reshape.7
  656.5 8.7 maximum_bitcast_fusion
  665.3 6.2 reshape.714
  672.8 23.1 %fusion.12 = (f32[9216,20]{0,1:T(8,128)S(1)}, f32[9216,20]{0,1:T(8,128)S(1)}, f32[9216,20]{0,1:T(8,128)S(1)}, f32[9216,20]{0,1:T(8,128)}) fusion(f32[9216,20]{0,1:T(8,128)S(1)} %bitcast_convert_fusion.5, bf16[1,20,20,9216]{3,0,2,1:T(2,128)(2,1)} %get-tuple-element.25, f32[9216,20]{0,1:T(8,128)S(1)} %bitcast_convert_fusion.4, ...), kind=kLoop, calls=%fused_computation.23 | loop fusion | flops 36126720 | bytes 19169280 | tf_op jit(solution)/shard_map/sok,iok->sik/dot_general | solution.py:201
  712.1 6.4 copy.147
  718.5 6.4 reshape.717
  747.5 53.1 %all-to-all-done.5 = bf16[1,16,64,1280]{3,1,0,2:T(8,128)(2,1)} async-done(((bf16[1,16,64,1280]{3,1,0,2:T(8,128)(2,1)}), bf16[1,16,64,1280]{3,1,0,2:T(8,128)(2,1)}, u32[]{:S(2)}, u32[]{:S(2)}) %all-to-all-start.5) | async-done | bytes 2621472 | tf_op jit(solution)/shard_map/all_to_all | solution.py:140
  805.0 8.8 reshape.772
  813.8 20.4 %fusion.129 = f32[512,8,1280]{0,2,1:T(8,128)} fusion(bf16[1280,1280,1]{1,0,2:T(8,128)(2,1)S(1)} %reshape.772, bf16[512,8,1280]{0,2,1:T(8,128)(2,1)} %copy-done), kind=kOutput, calls=%fused_computation.239 | convolution fusion | flops 13421772800 | bytes 34734080 | tf_op jit(solution)/shard_map/szxR,rR->szxr/dot_general | solution.py:210
  837.0 28.3 %all-to-all-done.4 = bf16[1,16,64,1280]{3,1,0,2:T(8,128)(2,1)} async-done(((bf16[1,16,64,1280]{3,1,0,2:T(8,128)(2,1)}), bf16[1,16,64,1280]{3,1,0,2:T(8,128)(2,1)}, u32[]{:S(2)}, u32[]{:S(2)}) %all-to-all-start.4) | async-done | bytes 2621472 | tf_op jit(solution)/shard_map/all_to_all | solution.py:139
  868.0 8.7 fusion.41
  876.7 18.5 %fusion.6 = bf16[1,512,8,1280]{1,3,2,0:T(8,128)(2,1)} fusion(f32[512,8,1280]{0,2,1:T(8,128)} %fusion.129, f32[8,1280,512]{2,1,0:T(8,128)} %fusion.41, bf16[128,8,1280]{2,1,0:T(8,128)(2,1)S(1)} %bitcast.516, bf16[128,2,512]{2,0,1:T(8,128)(2,1)S(1)} %copy-done.16), kind=kOutput, calls=%fused_computation.16 | convolution fusion | flops 1357905920 | bytes 55181312 | tf_op jit(solution)/shard_map/mz,smxr->szxr/dot_general | solution.py:148
  895.1 16.8 %copy.160 = bf16[1,512,8,1280]{3,2,1,0:T(8,128)(2,1)} copy(bf16[1,512,8,1280]{1,3,2,0:T(8,128)(2,1)} %fusion.6) | data formatting | bytes 20971520
  912.0 9.1 copy.161
  (160 shorter events, 270.7 us)
Async XLA Ops:
  21.8 0.7 copy-start.15
  63.6 122.9 %all-to-all-start = ((bf16[8,1,16,2,8,1280]{5,3,2,4,1,0:T(2,128)(2,1)}), bf16[8,1,16,2,8,1280]{5,3,2,4,1,0:T(2,128)(2,1)}, u32[]{:S(2)}, u32[]{:S(2)}) async-start(bf16[8,1,16,2,8,1280]{5,3,2,4,1,0:T(2,128)(2,1)} %fusion.75), calls=%async_computation | async-start | bytes 10485760 | tf_op jit(solution)/shard_map/all_to_all | solution.py:128
  186.5 5.5 copy-start.1
  192.0 5.9 copy-start.11
  192.0 3.0 copy-start.3
  195.0 2.9 copy-start.2
  276.0 5.8 copy-start.7
  279.4 1.0 copy-start.10
  286.3 64.7 %all-to-all-start.2 = ((bf16[1,16,64,1280]{3,1,0,2:T(8,128)(2,1)}), bf16[1,16,64,1280]{3,1,0,2:T(8,128)(2,1)}, u32[]{:S(2)}, u32[]{:S(2)}) async-start(bf16[1,16,64,1280]{3,1,0,2:T(8,128)(2,1)} %copy.136), calls=%async_computation.2 | async-start | bytes 5242880 | tf_op jit(solution)/shard_map/all_to_all | solution.py:140
  290.7 2.9 copy-start.4
  295.1 60.8 %copy-start.18 = (bf16[20,20]{1,0:T(8,128)(2,1)S(1)}, bf16[20,20]{1,0:T(8,128)(2,1)}, u32[]{:S(2)}) copy-start(bf16[20,20]{1,0:T(8,128)(2,1)} %param.8) | copy-start | bytes 2404
  295.1 60.8 %copy-start.19 = (bf16[20]{0:T(256)(128)(2,1)S(1)}, bf16[20]{0:T(256)(128)(2,1)}, u32[]{:S(2)}) copy-start(bf16[20]{0:T(256)(128)(2,1)} %param.9) | copy-start | bytes 124
  295.2 60.9 %copy-start.17 = (bf16[128,2,512]{2,0,1:T(8,128)(2,1)S(1)}, bf16[128,2,512]{2,0,1:T(8,128)(2,1)}, u32[]{:S(2)}) copy-start(bf16[128,2,512]{2,0,1:T(8,128)(2,1)} %get-tuple-element.36) | copy-start | bytes 786436
  351.0 65.2 %all-to-all-start.1 = ((bf16[1,16,64,1280]{3,1,0,2:T(8,128)(2,1)}), bf16[1,16,64,1280]{3,1,0,2:T(8,128)(2,1)}, u32[]{:S(2)}, u32[]{:S(2)}) async-start(bf16[1,16,64,1280]{3,1,0,2:T(8,128)(2,1)} %copy.132), calls=%async_computation.1 | async-start | bytes 5242880 | tf_op jit(solution)/shard_map/all_to_all | solution.py:139
  449.0 4.1 copy-start
  488.2 121.1 %all-to-all-start.3 = ((bf16[8,1,16,2,8,1280]{5,3,2,4,1,0:T(2,128)(2,1)}), bf16[8,1,16,2,8,1280]{5,3,2,4,1,0:T(2,128)(2,1)}, u32[]{:S(2)}, u32[]{:S(2)}) async-start(bf16[8,1,16,2,8,1280]{5,3,2,4,1,0:T(2,128)(2,1)} %fusion.67), calls=%async_computation.3 | async-start | bytes 10485760 | tf_op jit(solution)/shard_map/all_to_all | solution.py:128
  492.9 419.1 %reduce-scatter.2.cloned.1.call-start = ((), (), s32[]{:S(2)}) async-start(), calls=%async_computation.7 | async-start | bytes 22118400 | tf_op jit(solution)/shard_map/reduce_scatter | solution.py:213
  609.3 5.5 copy-start.5
  614.8 3.1 copy-start.12
  649.5 1.3 copy-start.13
  649.5 1.4 copy-start.14
  725.0 5.8 copy-start.8
  728.3 1.0 copy-start.9
  735.3 7.7 copy-start.6
  735.3 65.3 %all-to-all-start.5 = ((bf16[1,16,64,1280]{3,1,0,2:T(8,128)(2,1)}), bf16[1,16,64,1280]{3,1,0,2:T(8,128)(2,1)}, u32[]{:S(2)}, u32[]{:S(2)}) async-start(bf16[1,16,64,1280]{3,1,0,2:T(8,128)(2,1)} %copy.152), calls=%async_computation.5 | async-start | bytes 5242880 | tf_op jit(solution)/shard_map/all_to_all | solution.py:140
  800.6 64.7 %all-to-all-start.4 = ((bf16[1,16,64,1280]{3,1,0,2:T(8,128)(2,1)}), bf16[1,16,64,1280]{3,1,0,2:T(8,128)(2,1)}, u32[]{:S(2)}, u32[]{:S(2)}) async-start(bf16[1,16,64,1280]{3,1,0,2:T(8,128)(2,1)} %copy.148), calls=%async_computation.4 | async-start | bytes 5242880 | tf_op jit(solution)/shard_map/all_to_all | solution.py:139
  836.9 31.1 %copy-start.16 = (bf16[128,2,512]{2,0,1:T(8,128)(2,1)S(1)}, bf16[128,2,512]{2,0,1:T(8,128)(2,1)}, u32[]{:S(2)}) copy-start(bf16[128,2,512]{2,0,1:T(8,128)(2,1)} %copy-done.15) | copy-start | bytes 786436
Sparse Core Ops, SparseCore 0:
  665.4 160.1 reduce-scatter.1
